TPU v7x, 32 devices: a whole 2x2x4 slice. The times are simulated.
32 devices in a mesh: group: 4 (over y, x), leaf: 8 (over z, core).
Axes of the slice: x: 2, y: 2, z: 4, core: 2. Of those that a mesh axis runs over, the one named last changes fastest.
Arguments:
- points: bfloat16 [65536, 64], P(('group', 'leaf')), may hold values from -1.1953125 to 1.1953125
- ordering: int32 [32, 2048], P(('group', 'leaf')), may hold values from 0 to 2047, each once within a row
- iterate: float32 [65536, 128], P(('group', 'leaf')), may hold values from -6 to 6
- target: float32 [65536, 128], P(('group', 'leaf')), may hold values from -18 to 18
- step_size: float32 [128], replicated, may hold values from 0.1 to 0.5
- leaf_basis: bfloat16 [65536, 256], P(('group', 'leaf')), may hold values from -0.125 to 0.125
- transfer: bfloat16 [32, 256, 256], P(('group', 'leaf')), may hold values from -0.375 to 0.375
- leaf_skeleton: bfloat16 [32, 256, 64], P(('group', 'leaf')), may hold values from -0.8984375 to 0.8984375
- cluster_skeleton: bfloat16 [4, 256, 64], P('group'), may hold values from -1.1953125 to 1.1953125
- near_table: int32 [32, 8], P(('group', 'leaf')), may hold values from 0 to 1, as said below
- far_table: int32 [32, 8], P(('group', 'leaf')), may hold values from 0 to 1, as said below
- cluster_far: int32 [4, 4], P('group'), may hold values from 0 to 1, as said below
Outputs:
- updated: float32 [65536, 128], P(('group', 'leaf'))
Inputs may be any that keep to these rules, and one draw needn't show every extreme that they name: `near_table`: entries 0 or 1; each leaf's own place is 1; a 1 stands only at places at most 3 away from the leaf's own place; each row has at most 7 ones, and some row exactly 7. `far_table`: entries 0 or 1, never 1 where near_table is 1. `cluster_far`: entries 0 or 1, zero on the diagonal. `ordering`: each row is a permutation.
All inputs are finite; a program needn't handle non-finite values.
Results may differ from a plain program's by a relative error of at most 0.0044.
Values may be sent and summed in bfloat16 or wider, within the bound.
No kernel may reach another device: no remote copies, remote signals or barrier semaphores. Data moves between devices by JAX's collectives and lax.ppermute only.
A program may use at most 128 MiB of HBM per device.

v0:
```python
import jax
import jax.numpy as jnp
from jax import lax
from jax.sharding import PartitionSpec as P

NEAR_MOST = 7


def passed_along(block, axis, distance):
    devices = range(lax.axis_size(axis))
    route = [(i - distance, i) for i in devices if i - distance in devices]
    return lax.ppermute(block, axis, route)


def kernel_tile(left, right):
    left_f = left.astype(jnp.float32)
    right_f = right.astype(jnp.float32)
    left_sq = jnp.sum(left_f * left_f, axis=1)
    right_sq = jnp.sum(right_f * right_f, axis=1)
    inner = lax.dot_general(
        left, right, (((1,), (1,)), ((), ())), preferred_element_type=jnp.float32
    )
    return jnp.exp(-(left_sq[:, None] + right_sq[None, :] - 2.0 * inner)).astype(jnp.bfloat16)


def body(
    points,
    ordering,
    iterate,
    target,
    step_size,
    leaf_basis,
    transfer,
    leaf_skeleton,
    cluster_skeleton,
    near_table,
    far_table,
    cluster_far,
):
    leaf_rows = points.shape[0]
    point_cols = points.shape[1]
    rhs_cols = iterate.shape[1]
    rank_cols = leaf_basis.shape[1]
    rounded = iterate.astype(jnp.bfloat16)
    coeffs = lax.dot_general(
        leaf_basis, rounded, (((0,), (0,)), ((), ())), preferred_element_type=jnp.float32
    ).astype(jnp.bfloat16)
    near_row = near_table[0]
    far_row = far_table[0]
    own_transfer = transfer[0]
    reach = (NEAR_MOST - 1) // 2
    joined = jnp.concatenate([points, rounded], axis=1)
    below_blocks = []
    above_blocks = []
    passing_below = joined
    passing_above = joined
    for distance in range(1, reach + 1):
        passing_below = passed_along(passing_below, "leaf", 1)
        passing_above = passed_along(passing_above, "leaf", -1)
        below_blocks.append(passing_below)
        above_blocks.append(passing_above)
    padded = jnp.concatenate(below_blocks[::-1] + [joined] + above_blocks, axis=0)
    myself = lax.axis_index("leaf")
    cluster_size = near_row.shape[0]

    def window_visit(position, summed):
        place = myself + position - reach
        inside = (place >= 0) & (place < cluster_size)
        listed = lax.dynamic_index_in_dim(
            near_row, jnp.clip(place, 0, cluster_size - 1), 0, keepdims=False
        )
        block = lax.dynamic_slice_in_dim(padded, position * leaf_rows, leaf_rows, 0)
        other_points = block[:, :point_cols]
        other_values = block[:, point_cols:]

        def include(current):
            return current + jnp.dot(
                kernel_tile(points, other_points), other_values, preferred_element_type=jnp.float32
            )

        return lax.cond(inside & (listed > 0), include, lambda current: current, summed)

    near_sum = lax.fori_loop(
        0, 2 * reach + 1, window_visit, jnp.zeros((leaf_rows, rhs_cols), jnp.float32)
    )

    def far_visit(skeletons, values):

        def visit(position, summed):
            listed = lax.dynamic_index_in_dim(far_row, position, 0, keepdims=False)

            def include(current):
                return current + jnp.dot(
                    kernel_tile(leaf_skeleton[0], skeletons[position]),
                    values[position],
                    preferred_element_type=jnp.float32,
                )

            return lax.cond(listed > 0, include, lambda current: current, summed)

        return visit

    empty_far = jnp.zeros((rank_cols, rhs_cols), jnp.float32)
    skeletons = lax.all_gather(leaf_skeleton, "leaf", axis=0, tiled=True)
    values = lax.all_gather(coeffs[None], "leaf", axis=0, tiled=True)
    far_sum = lax.fori_loop(0, skeletons.shape[0], far_visit(skeletons, values), empty_far)
    upward_terms = lax.dot_general(
        own_transfer, coeffs, (((0,), (0,)), ((), ())), preferred_element_type=jnp.float32
    )
    upper = lax.psum(upward_terms, "leaf").astype(jnp.bfloat16)
    cluster_row = cluster_far[0]
    skeletons = lax.all_gather(cluster_skeleton, "group", axis=0, tiled=True)
    values = lax.all_gather(upper[None], "group", axis=0, tiled=True)

    def visit(position, summed):
        listed = lax.dynamic_index_in_dim(cluster_row, position, 0, keepdims=False)

        def include(current):
            return current + jnp.dot(
                kernel_tile(cluster_skeleton[0], skeletons[position]),
                values[position],
                preferred_element_type=jnp.float32,
            )

        return lax.cond(listed > 0, include, lambda current: current, summed)

    lower = lax.fori_loop(0, skeletons.shape[0], visit, empty_far).astype(jnp.bfloat16)
    local = (far_sum + jnp.dot(own_transfer, lower, preferred_element_type=jnp.float32)).astype(
        jnp.bfloat16
    )
    image = jnp.dot(leaf_basis, local, preferred_element_type=jnp.float32) + near_sum
    sorted_target = target[ordering[0]]
    return iterate + step_size[None, :] * (sorted_target - image)


def solution(mesh):
    return jax.shard_map(
        body,
        mesh=mesh,
        in_specs=(
            P(("group", "leaf"), None),
            P(("group", "leaf"), None),
            P(("group", "leaf"), None),
            P(("group", "leaf"), None),
            P(),
            P(("group", "leaf"), None),
            P(("group", "leaf"), None, None),
            P(("group", "leaf"), None, None),
            P("group", None, None),
            P(("group", "leaf"), None),
            P(("group", "leaf"), None),
            P("group", None),
        ),
        out_specs=P(("group", "leaf"), None),
        check_vma=False,
    )
```

profile of v0, /device:TPU:15, one launch (start us, length us, event | category | flops | bytes accessed | tf_op | source)
XLA Modules:
  0.0 278.6 jit_solution(15546868874311557150)
XLA Ops:
  4.6 3.9 %collective-permute-start = (bf16[2048,192]{0,1:T(8,128)(2,1)}, bf16[2048,192]{0,1:T(8,128)(2,1)}, u32[]{:S(2)}, u32[]{:S(2)}) collective-permute-start(bf16[2048,192]{0,1:T(8,128)(2,1)} %pad_maximum_fusion), channel_id=1, source_target_pairs={{0,1},{1,2},{2,3},{3,4},{4,5},{5,6},{6,7},{8,9},{9,10},{10,11},{11... | collective-permute-start | bytes 2359304 | tf_op jit(solution)/shard_map/ppermute | solution.py:12
  10.4 7.3 %collective-permute-done = bf16[2048,192]{0,1:T(8,128)(2,1)} collective-permute-done((bf16[2048,192]{0,1:T(8,128)(2,1)}, bf16[2048,192]{0,1:T(8,128)(2,1)}, u32[]{:S(2)}, u32[]{:S(2)}) %collective-permute-start) | collective-permute-done | bytes 786464 | tf_op jit(solution)/shard_map/ppermute | solution.py:12
  17.7 4.4 %collective-permute-start.1 = (bf16[2048,192]{0,1:T(8,128)(2,1)}, bf16[2048,192]{0,1:T(8,128)(2,1)}, u32[]{:S(2)}, u32[]{:S(2)}) collective-permute-start(bf16[2048,192]{0,1:T(8,128)(2,1)} %collective-permute-done), channel_id=1, source_target_pairs={{0,1},{1,2},{2,3},{3,4},{4,5},{5,6},{6,7},{8,9},{9,10},{10,11},{11... | collective-permute-start | bytes 2359304 | tf_op jit(solution)/shard_map/ppermute | solution.py:12
  22.8 25.1 %all-reduce.1 = bf16[256,128]{0,1:T(8,128)(2,1)S(1)} all-reduce(f32[256,128]{0,1:T(8,128)S(1)} %convolution_bitcast_fusion.2), channel_id=1, replica_groups=mesh['group'=4,'leaf'=8] {'leaf'}, use_global_device_ids=true, to_apply=%region_6.7 | all-reduce | flops 32768 | bytes 196608 | tf_op jit(solution)/shard_map/psum | solution.py:110
  47.9 17.8 %all-gather = bf16[2048,128]{1,0:T(8,128)(2,1)} all-gather(bf16[256,128]{1,0:T(8,128)(2,1)S(1)} %convolution_convert_fusion), channel_id=2, replica_groups=mesh['group'=4,'leaf'=8] {'leaf'}, dimensions={0}, use_global_device_ids=true | all-gather | bytes 589824 | tf_op jit(solution)/shard_map/all_gather | solution.py:105
  67.8 4.1 %collective-permute-start.2 = (bf16[2048,192]{0,1:T(8,128)(2,1)}, bf16[2048,192]{0,1:T(8,128)(2,1)}, u32[]{:S(2)}, u32[]{:S(2)}) collective-permute-start(bf16[2048,192]{0,1:T(8,128)(2,1)} %collective-permute-done.1), channel_id=1, source_target_pairs={{0,1},{1,2},{2,3},{3,4},{4,5},{5,6},{6,7},{8,9},{9,10},{10,11},{11... | collective-permute-start | bytes 2359304 | tf_op jit(solution)/shard_map/ppermute | solution.py:12
  71.9 20.0 %all_gather.12 = bf16[8,256,64]{1,2,0:T(8,128)(2,1)} all-gather(bf16[1,256,64]{1,2,0:T(8,128)(2,1)S(1)} %copy-done.8), channel_id=1, replica_groups=mesh['group'=4,'leaf'=8] {'leaf'}, dimensions={0}, use_global_device_ids=true | all-gather | bytes 294912 | tf_op jit(solution)/shard_map/all_gather | solution.py:104
  95.7 17.8 %while.50 = (s32[]{:T(128)}, f32[256,128]{1,0:T(8,128)}, s32[8]{0:T(128)}, bf16[1,256,64]{2,1,0:T(8,128)(2,1)S(1)}, bf16[8,256,64]{2,1,0:T(8,128)(2,1)}, /*index...) while((s32[]{:T(128)}, f32[256,128]{1,0:T(8,128)}, s32[8]{0:T(128)}, bf16[1,256,64]{2,1,0:T(8,128)(2,1)S(1)}, ...), condition=%wide.region_5.6_spmd, body=%wide.region_0.5_spmd.sunk | while | flops 25624072 | bytes 496837 | solution.py:106
  110.4 3.1 %conditional.6 = (f32[256,128]{1,0:T(8,128)}) conditional(s32[]{:T(128)} %bitcast.109, f32[256,128]{1,0:T(8,128)} %get-tuple-element.740, (bf16[1,256,64]{2,1,0:T(8,128)(2,1)S(1)}, s32[]{:T(128)}, bf16[8,256,64]{2,1,0:T(8,128)(2,1)}, bf16[8,256,128]{2,1,0:T(8,128)(2,1)}, f32[256,128]{1,0:T(8,128)}) %tuple.135), branch_computations={%region_1.1_spmd, %region_2.4_spmd} | conditional | flops 25624068 | bytes 496686 | solution.py:99
  115.2 13.8 %all-gather.1 = bf16[1024,128]{0,1:T(8,128)(2,1)} all-gather(bf16[256,128]{0,1:T(8,128)(2,1)S(1)} %all-reduce.1), channel_id=3, replica_groups=mesh['group'=4,'leaf'=8] {'group'}, dimensions={0}, use_global_device_ids=true | all-gather | bytes 327680 | tf_op jit(solution)/shard_map/all_gather | solution.py:113
  131.6 7.2 %all_gather.14 = bf16[4,256,64]{1,2,0:T(8,128)(2,1)} all-gather(bf16[1,256,64]{1,2,0:T(8,128)(2,1)} %param.32), channel_id=1, replica_groups=mesh['group'=4,'leaf'=8] {'group'}, dimensions={0}, use_global_device_ids=true | all-gather | bytes 163840 | tf_op jit(solution)/shard_map/all_gather | solution.py:112
  140.6 7.6 %gather_fusion = f32[2048,128]{1,0:T(8,128)} fusion(f32[2048,128]{1,0:T(8,128)S(1)} %copy-done.1, s32[2048]{0:T(1024)S(1)} %broadcast_clamp_fusion), kind=kCustom, calls=%fused_computation | custom fusion | bytes 2105344 | tf_op jit(solution)/shard_map/gather | solution.py:132
  148.2 2.6 copy.45
  150.8 9.8 %while.51 = (s32[]{:T(128)}, f32[256,128]{1,0:T(8,128)S(1)}, s32[4]{0:T(128)S(1)}, bf16[1,256,64]{2,1,0:T(8,128)(2,1)S(1)}, bf16[4,256,64]{2,1,0:T(8,128)(2,1)},...) while((s32[]{:T(128)}, f32[256,128]{1,0:T(8,128)S(1)}, s32[4]{0:T(128)S(1)}, ...), condition=%wide.region_12.13_spmd, body=%wide.region_7.12_spmd.sunk | while | flops 25624072 | bytes 496837 | solution.py:127
  160.7 9.4 %collective-permute-start.5 = (bf16[2048,192]{0,1:T(8,128)(2,1)}, bf16[2048,192]{0,1:T(8,128)(2,1)S(1)}, u32[]{:S(2)}, u32[]{:S(2)}) collective-permute-start(bf16[2048,192]{0,1:T(8,128)(2,1)} %collective-permute-done.4), channel_id=1, source_target_pairs={{1,0},{2,1},{3,2},{4,3},{5,4},{6,5},{7,6},{9,8},{10,9},{11,10},{12... | collective-permute-start | bytes 2359304 | tf_op jit(solution)/shard_map/ppermute | solution.py:12
  182.8 9.2 %copy.43 = bf16[14336,192]{1,0:T(8,128)(2,1)} copy(bf16[14336,192]{0,1:T(8,128)(2,1)} %constant_dynamic-update-slice_fusion) | data formatting | bytes 11010048 | tf_op jit(solution)/shard_map/while | solution.py:83
  193.2 77.1 %while.52 = (s32[]{:T(128)}, f32[2048,128]{1,0:T(8,128)}, s32[]{:T(128)}, s32[8]{0:T(128)S(1)}, bf16[2048,64]{1,0:T(8,128)(2,1)S(1)}, /*index=5*/bf16[14336,192]...) while((s32[]{:T(128)}, f32[2048,128]{1,0:T(8,128)}, ...), condition=%wide.region_18.19_spmd, body=%wide.region_13.18_spmd.sunk | while | flops 1632628736 | bytes 3966781 | solution.py:83
  194.5 9.7 %conditional.8 = (f32[2048,128]{1,0:T(8,128)}) conditional(s32[]{:T(128)} %convert_element_type.116, f32[2048,128]{1,0:T(8,128)} %get-tuple-element.708, (bf16[2048,64]{1,0:T(8,128)(2,1)S(1)}, s32[]{:T(128)}, bf16[14336,192]{1,0:T(8,128)(2,1)}, f32[2048,128]{1,0:T(8,128)}) %tuple.139), branch_computations={%region_14.14_spmd, %region_15.17_spmd} | conditional | flops 1632628736 | bytes 3966534 | solution.py:81
  196.2 8.0 %convolution_add_fusion = f32[2048,128]{1,0:T(8,128)} fusion(f32[2048,128]{1,0:T(8,128)} %get-tuple-element.471, bf16[2048,64]{1,0:T(8,128)(2,1)S(1)} %get-tuple-element.472, f32[2048]{0:T(1024)S(1)} %get-tuple-element.582, f32[2048]{0:T(1024)S(1)} %get-tuple-element.583, bf16[14336,192]{1,0:T(8,128)(2,1)} %get-tuple-element.473, s32[]{:T(128)S(6)} %select_n.45, ...), kind=kOutput, calls=%fused_computation.47 | convolution fusion | flops 1631846400 | bytes 3425792 | tf_op jit(solution)/shard_map/while/body/eval_jaxpr/cond/branch_1_fun/dot_general | solution.py:77
  205.5 9.7 %conditional.8 = (f32[2048,128]{1,0:T(8,128)}) conditional(s32[]{:T(128)} %convert_element_type.116, f32[2048,128]{1,0:T(8,128)} %get-tuple-element.708, (bf16[2048,64]{1,0:T(8,128)(2,1)S(1)}, s32[]{:T(128)}, bf16[14336,192]{1,0:T(8,128)(2,1)}, f32[2048,128]{1,0:T(8,128)}) %tuple.139), branch_computations={%region_14.14_spmd, %region_15.17_spmd} | conditional | flops 1632628736 | bytes 3966534 | solution.py:81
  207.2 8.0 %convolution_add_fusion = f32[2048,128]{1,0:T(8,128)} fusion(f32[2048,128]{1,0:T(8,128)} %get-tuple-element.471, bf16[2048,64]{1,0:T(8,128)(2,1)S(1)} %get-tuple-element.472, f32[2048]{0:T(1024)S(1)} %get-tuple-element.582, f32[2048]{0:T(1024)S(1)} %get-tuple-element.583, bf16[14336,192]{1,0:T(8,128)(2,1)} %get-tuple-element.473, s32[]{:T(128)S(6)} %select_n.45, ...), kind=kOutput, calls=%fused_computation.47 | convolution fusion | flops 1631846400 | bytes 3425792 | tf_op jit(solution)/shard_map/while/body/eval_jaxpr/cond/branch_1_fun/dot_general | solution.py:77
  216.5 9.7 %conditional.8 = (f32[2048,128]{1,0:T(8,128)}) conditional(s32[]{:T(128)} %convert_element_type.116, f32[2048,128]{1,0:T(8,128)} %get-tuple-element.708, (bf16[2048,64]{1,0:T(8,128)(2,1)S(1)}, s32[]{:T(128)}, bf16[14336,192]{1,0:T(8,128)(2,1)}, f32[2048,128]{1,0:T(8,128)}) %tuple.139), branch_computations={%region_14.14_spmd, %region_15.17_spmd} | conditional | flops 1632628736 | bytes 3966534 | solution.py:81
  218.2 8.0 %convolution_add_fusion = f32[2048,128]{1,0:T(8,128)} fusion(f32[2048,128]{1,0:T(8,128)} %get-tuple-element.471, bf16[2048,64]{1,0:T(8,128)(2,1)S(1)} %get-tuple-element.472, f32[2048]{0:T(1024)S(1)} %get-tuple-element.582, f32[2048]{0:T(1024)S(1)} %get-tuple-element.583, bf16[14336,192]{1,0:T(8,128)(2,1)} %get-tuple-element.473, s32[]{:T(128)S(6)} %select_n.45, ...), kind=kOutput, calls=%fused_computation.47 | convolution fusion | flops 1631846400 | bytes 3425792 | tf_op jit(solution)/shard_map/while/body/eval_jaxpr/cond/branch_1_fun/dot_general | solution.py:77
  227.5 9.7 %conditional.8 = (f32[2048,128]{1,0:T(8,128)}) conditional(s32[]{:T(128)} %convert_element_type.116, f32[2048,128]{1,0:T(8,128)} %get-tuple-element.708, (bf16[2048,64]{1,0:T(8,128)(2,1)S(1)}, s32[]{:T(128)}, bf16[14336,192]{1,0:T(8,128)(2,1)}, f32[2048,128]{1,0:T(8,128)}) %tuple.139), branch_computations={%region_14.14_spmd, %region_15.17_spmd} | conditional | flops 1632628736 | bytes 3966534 | solution.py:81
  229.2 8.0 %convolution_add_fusion = f32[2048,128]{1,0:T(8,128)} fusion(f32[2048,128]{1,0:T(8,128)} %get-tuple-element.471, bf16[2048,64]{1,0:T(8,128)(2,1)S(1)} %get-tuple-element.472, f32[2048]{0:T(1024)S(1)} %get-tuple-element.582, f32[2048]{0:T(1024)S(1)} %get-tuple-element.583, bf16[14336,192]{1,0:T(8,128)(2,1)} %get-tuple-element.473, s32[]{:T(128)S(6)} %select_n.45, ...), kind=kOutput, calls=%fused_computation.47 | convolution fusion | flops 1631846400 | bytes 3425792 | tf_op jit(solution)/shard_map/while/body/eval_jaxpr/cond/branch_1_fun/dot_general | solution.py:77
  238.5 9.7 %conditional.8 = (f32[2048,128]{1,0:T(8,128)}) conditional(s32[]{:T(128)} %convert_element_type.116, f32[2048,128]{1,0:T(8,128)} %get-tuple-element.708, (bf16[2048,64]{1,0:T(8,128)(2,1)S(1)}, s32[]{:T(128)}, bf16[14336,192]{1,0:T(8,128)(2,1)}, f32[2048,128]{1,0:T(8,128)}) %tuple.139), branch_computations={%region_14.14_spmd, %region_15.17_spmd} | conditional | flops 1632628736 | bytes 3966534 | solution.py:81
  240.2 8.0 %convolution_add_fusion = f32[2048,128]{1,0:T(8,128)} fusion(f32[2048,128]{1,0:T(8,128)} %get-tuple-element.471, bf16[2048,64]{1,0:T(8,128)(2,1)S(1)} %get-tuple-element.472, f32[2048]{0:T(1024)S(1)} %get-tuple-element.582, f32[2048]{0:T(1024)S(1)} %get-tuple-element.583, bf16[14336,192]{1,0:T(8,128)(2,1)} %get-tuple-element.473, s32[]{:T(128)S(6)} %select_n.45, ...), kind=kOutput, calls=%fused_computation.47 | convolution fusion | flops 1631846400 | bytes 3425792 | tf_op jit(solution)/shard_map/while/body/eval_jaxpr/cond/branch_1_fun/dot_general | solution.py:77
  249.5 9.7 %conditional.8 = (f32[2048,128]{1,0:T(8,128)}) conditional(s32[]{:T(128)} %convert_element_type.116, f32[2048,128]{1,0:T(8,128)} %get-tuple-element.708, (bf16[2048,64]{1,0:T(8,128)(2,1)S(1)}, s32[]{:T(128)}, bf16[14336,192]{1,0:T(8,128)(2,1)}, f32[2048,128]{1,0:T(8,128)}) %tuple.139), branch_computations={%region_14.14_spmd, %region_15.17_spmd} | conditional | flops 1632628736 | bytes 3966534 | solution.py:81
  251.2 8.1 %convolution_add_fusion = f32[2048,128]{1,0:T(8,128)} fusion(f32[2048,128]{1,0:T(8,128)} %get-tuple-element.471, bf16[2048,64]{1,0:T(8,128)(2,1)S(1)} %get-tuple-element.472, f32[2048]{0:T(1024)S(1)} %get-tuple-element.582, f32[2048]{0:T(1024)S(1)} %get-tuple-element.583, bf16[14336,192]{1,0:T(8,128)(2,1)} %get-tuple-element.473, s32[]{:T(128)S(6)} %select_n.45, ...), kind=kOutput, calls=%fused_computation.47 | convolution fusion | flops 1631846400 | bytes 3425792 | tf_op jit(solution)/shard_map/while/body/eval_jaxpr/cond/branch_1_fun/dot_general | solution.py:77
  260.5 9.8 %conditional.8 = (f32[2048,128]{1,0:T(8,128)}) conditional(s32[]{:T(128)} %convert_element_type.116, f32[2048,128]{1,0:T(8,128)} %get-tuple-element.708, (bf16[2048,64]{1,0:T(8,128)(2,1)S(1)}, s32[]{:T(128)}, bf16[14336,192]{1,0:T(8,128)(2,1)}, f32[2048,128]{1,0:T(8,128)}) %tuple.139), branch_computations={%region_14.14_spmd, %region_15.17_spmd} | conditional | flops 1632628736 | bytes 3966534 | solution.py:81
  262.2 8.1 %convolution_add_fusion = f32[2048,128]{1,0:T(8,128)} fusion(f32[2048,128]{1,0:T(8,128)} %get-tuple-element.471, bf16[2048,64]{1,0:T(8,128)(2,1)S(1)} %get-tuple-element.472, f32[2048]{0:T(1024)S(1)} %get-tuple-element.582, f32[2048]{0:T(1024)S(1)} %get-tuple-element.583, bf16[14336,192]{1,0:T(8,128)(2,1)} %get-tuple-element.473, s32[]{:T(128)S(6)} %select_n.45, ...), kind=kOutput, calls=%fused_computation.47 | convolution fusion | flops 1631846400 | bytes 3425792 | tf_op jit(solution)/shard_map/while/body/eval_jaxpr/cond/branch_1_fun/dot_general | solution.py:77
  272.9 3.2 %fusion.56 = f32[2048,128]{0,1:T(8,128)} fusion(f32[2048,128]{0,1:T(8,128)S(1)} %copy-done.3, f32[2048,128]{0,1:T(8,128)} %copy.45, f32[2048,128]{0,1:T(8,128)} %copy.44, bf16[2048,256]{1,0:T(8,128)(2,1)S(1)} %copy-done, f32[256,128]{0,1:T(8,128)S(1)} %copy-done.7, f32[128]{0:T(128)S(1)} %copy-done.10, bf16[1,256,256]{2,1,0:T(8,128)(2,1)S(1)} %copy-done.6, ...), kind=kOutput, calls=%fused_computation.58 | convolution fusion | flops 152141824 | bytes 5636608 | tf_op jit(solution)/shard_map/dot_general | solution.py:131
  (102 shorter events, 78.9 us)
Async XLA Ops:
  0.0 22.1 %copy-start = (bf16[2048,256]{1,0:T(8,128)(2,1)S(1)}, bf16[2048,256]{1,0:T(8,128)(2,1)}, u32[]{:S(2)}) copy-start(bf16[2048,256]{1,0:T(8,128)(2,1)} %param.29) | copy-start | bytes 3145732
  0.0 91.9 %copy-start.4 = (bf16[2048,64]{0,1:T(8,128)(2,1)S(1)}, bf16[2048,64]{0,1:T(8,128)(2,1)}, u32[]{:S(2)}) copy-start(bf16[2048,64]{0,1:T(8,128)(2,1)} %param.24) | copy-start | bytes 786436
  0.0 22.6 %copy-start.5 = (bf16[1,256,256]{2,1,0:T(8,128)(2,1)S(1)}, bf16[1,256,256]{2,1,0:T(8,128)(2,1)}, u32[]{:S(2)}) copy-start(bf16[1,256,256]{2,1,0:T(8,128)(2,1)} %param.30) | copy-start | bytes 393220
  0.0 71.9 %copy-start.8 = (bf16[1,256,64]{1,2,0:T(8,128)(2,1)S(1)}, bf16[1,256,64]{1,2,0:T(8,128)(2,1)}, u32[]{:S(2)}) copy-start(bf16[1,256,64]{1,2,0:T(8,128)(2,1)} %param.31) | copy-start | bytes 98308
  1.7 1.0 copy-start.2
  2.7 137.9 %copy-start.9 = (s32[1,2048]{1,0:T(1,128)S(1)}, s32[1,2048]{1,0:T(1,128)}, u32[]{:S(2)}) copy-start(s32[1,2048]{1,0:T(1,128)} %param.25) | copy-start | bytes 24580
  4.6 136.0 %copy-start.1 = (f32[2048,128]{1,0:T(8,128)S(1)}, f32[2048,128]{1,0:T(8,128)}, u32[]{:S(2)}) copy-start(f32[2048,128]{1,0:T(8,128)} %param.27) | copy-start | bytes 3145732
  4.6 13.1 %collective-permute-start = (bf16[2048,192]{0,1:T(8,128)(2,1)}, bf16[2048,192]{0,1:T(8,128)(2,1)}, u32[]{:S(2)}, u32[]{:S(2)}) collective-permute-start(bf16[2048,192]{0,1:T(8,128)(2,1)} %pad_maximum_fusion), channel_id=1, source_target_pairs={{0,1},{1,2},{2,3},{3,4},{4,5},{5,6},{6,7},{8,9},{9,10},{10,11},{11... | collective-permute-start | bytes 2359304 | tf_op jit(solution)/shard_map/ppermute | solution.py:12
  8.5 57.3 %collective-permute-start.3 = (bf16[2048,192]{0,1:T(8,128)(2,1)}, bf16[2048,192]{0,1:T(8,128)(2,1)}, u32[]{:S(2)}, u32[]{:S(2)}) collective-permute-start(bf16[2048,192]{0,1:T(8,128)(2,1)} %pad_maximum_fusion), channel_id=1, source_target_pairs={{1,0},{2,1},{3,2},{4,3},{5,4},{6,5},{7,6},{9,8},{10,9},{11,10},{12... | collective-permute-start | bytes 2359304 | tf_op jit(solution)/shard_map/ppermute | solution.py:12
  17.7 50.1 %collective-permute-start.1 = (bf16[2048,192]{0,1:T(8,128)(2,1)}, bf16[2048,192]{0,1:T(8,128)(2,1)}, u32[]{:S(2)}, u32[]{:S(2)}) collective-permute-start(bf16[2048,192]{0,1:T(8,128)(2,1)} %collective-permute-done), channel_id=1, source_target_pairs={{0,1},{1,2},{2,3},{3,4},{4,5},{5,6},{6,7},{8,9},{9,10},{10,11},{11... | collective-permute-start | bytes 2359304 | tf_op jit(solution)/shard_map/ppermute | solution.py:12
  65.8 94.9 %collective-permute-start.4 = (bf16[2048,192]{0,1:T(8,128)(2,1)}, bf16[2048,192]{0,1:T(8,128)(2,1)}, u32[]{:S(2)}, u32[]{:S(2)}) collective-permute-start(bf16[2048,192]{0,1:T(8,128)(2,1)} %collective-permute-done.3), channel_id=1, source_target_pairs={{1,0},{2,1},{3,2},{4,3},{5,4},{6,5},{7,6},{9,8},{10,9},{11,10},{12... | collective-permute-start | bytes 2359304 | tf_op jit(solution)/shard_map/ppermute | solution.py:12
  67.8 102.2 %collective-permute-start.2 = (bf16[2048,192]{0,1:T(8,128)(2,1)}, bf16[2048,192]{0,1:T(8,128)(2,1)}, u32[]{:S(2)}, u32[]{:S(2)}) collective-permute-start(bf16[2048,192]{0,1:T(8,128)(2,1)} %collective-permute-done.1), channel_id=1, source_target_pairs={{0,1},{1,2},{2,3},{3,4},{4,5},{5,6},{6,7},{8,9},{9,10},{10,11},{11... | collective-permute-start | bytes 2359304 | tf_op jit(solution)/shard_map/ppermute | solution.py:12
  140.6 10.2 %copy-start.11 = (s32[1,4]{1,0:T(1,128)S(1)}, s32[1,4]{1,0:T(1,128)}, u32[]{:S(2)}) copy-start(s32[1,4]{1,0:T(1,128)} %param.35) | copy-start | bytes 52
  160.7 21.2 %collective-permute-start.5 = (bf16[2048,192]{0,1:T(8,128)(2,1)}, bf16[2048,192]{0,1:T(8,128)(2,1)S(1)}, u32[]{:S(2)}, u32[]{:S(2)}) collective-permute-start(bf16[2048,192]{0,1:T(8,128)(2,1)} %collective-permute-done.4), channel_id=1, source_target_pairs={{1,0},{2,1},{3,2},{4,3},{5,4},{6,5},{7,6},{9,8},{10,9},{11,10},{12... | collective-permute-start | bytes 2359304 | tf_op jit(solution)/shard_map/ppermute | solution.py:12
  182.8 10.3 %copy-start.12 = (s32[1,8]{1,0:T(1,128)S(1)}, s32[1,8]{1,0:T(1,128)}, u32[]{:S(2)}) copy-start(s32[1,8]{1,0:T(1,128)} %param.33) | copy-start | bytes 100
  193.1 79.7 %copy-start.3 = (f32[2048,128]{0,1:T(8,128)S(1)}, f32[2048,128]{0,1:T(8,128)}, u32[]{:S(2)}) copy-start(f32[2048,128]{0,1:T(8,128)} %copy-done.2) | copy-start | bytes 3145732
  193.1 79.7 %copy-start.6 = (bf16[1,256,256]{2,1,0:T(8,128)(2,1)S(1)}, bf16[1,256,256]{2,1,0:T(8,128)(2,1)}, u32[]{:S(2)}) copy-start(bf16[1,256,256]{2,1,0:T(8,128)(2,1)} %param.30) | copy-start | bytes 393220
  193.1 79.7 %copy-start.7 = (f32[256,128]{0,1:T(8,128)S(1)}, f32[256,128]{0,1:T(8,128)}, u32[]{:S(2)}) copy-start(f32[256,128]{0,1:T(8,128)} %copy.41) | copy-start | bytes 393220
  193.2 79.7 %copy-start.10 = (f32[128]{0:T(128)S(1)}, f32[128]{0:T(128)}, u32[]{:S(2)}) copy-start(f32[128]{0:T(128)} %param.28) | copy-start | bytes 1540
where the time goes:
time: 281 us; the launch traced here: 279 us
  blocking collectives  84 us (30%)
  local copies, waits for them, and re-layouts  66.5 us (24%)
  matrix products  65 us (23%)
  starting transfers between devices  25.7 us (9%)
  other arithmetic  17.5 us (6%)
  loops' own time  12.3 us (4%)
  waiting for transfers between devices  7.31 us (3%)
    dot_general x7, matrix products, include(): jnp.dot(kernel_tile(points, other_points), other_values, preferred_elemen...  56.4 us
    ppermute x6, starting transfers between devices, passed_along(): return lax.ppermute(block, axis, route)  25.7 us
    psum x1, blocking collectives, body(): upper = lax.psum(upward_terms, 'leaf').astype(jnp.bfloat16)  25.1 us
    all_gather x1, blocking collectives, body(): skeletons = lax.all_gather(leaf_skeleton, 'leaf', axis=0, tiled=True)  20 us
    all_gather x1, blocking collectives, body(): values = lax.all_gather(coeffs[None], 'leaf', axis=0, tiled=True)  17.8 us
    reduce_sum x10, other arithmetic, kernel_tile(): right_sq = jnp.sum(right_f * right_f, axis=1)  14.6 us
    all_gather x1, blocking collectives, body(): values = lax.all_gather(upper[None], 'group', axis=0, tiled=True)  13.8 us
    unnamed x32, local copies, waits for them, and re-layouts  13.4 us
  transfers between devices with their start and end apart: 6, of which 1 were waited for; matrix products, arithmetic and copies ran while one was open for 19% of the time, Pallas kernels for 0%

commit v1 on v0

--- a/solution.py
+++ b/solution.py
@@ -2,6 +2,7 @@
 import jax.numpy as jnp
 from jax import lax
 from jax.sharding import PartitionSpec as P
+from jax.lax import axis_index, axis_size, ppermute
 
 NEAR_MOST = 7
 
@@ -101,7 +102,36 @@
         return visit
 
     empty_far = jnp.zeros((rank_cols, rhs_cols), jnp.float32)
-    skeletons = lax.all_gather(leaf_skeleton, "leaf", axis=0, tiled=True)
+    arr_next, current_value, q_next = (
+        axis_size("leaf"),
+        axis_index("leaf"),
+        leaf_skeleton.shape[0],
+    )
+    sheets = []
+    for c in tuple(range(arr_next)):
+        sheets.append((c, (c + 1) % arr_next))
+    vals = []
+    for c in tuple(range(arr_next)):
+        vals.append((c, (c - 1) % arr_next))
+    skeletons = jnp.zeros(
+        (*leaf_skeleton.shape[:0], arr_next * q_next, *leaf_skeleton.shape[0 + 1 :]),
+        leaf_skeleton.dtype,
+    )
+    skeletons = lax.dynamic_update_slice_in_dim(
+        skeletons, leaf_skeleton, current_value * q_next, axis=0
+    )
+    e_now = spare = leaf_skeleton
+    x_now = arr_next // 2
+    for p in [*range(1, x_now + 1)]:
+        e_now = ppermute(e_now, axis_name="leaf", perm=sheets)
+        skeletons = lax.dynamic_update_slice_in_dim(
+            skeletons, e_now, (current_value - p) % arr_next * q_next, axis=0
+        )
+        if p < arr_next - x_now:
+            spare = ppermute(spare, axis_name="leaf", perm=vals)
+            skeletons = lax.dynamic_update_slice_in_dim(
+                skeletons, spare, (current_value + p) % arr_next * q_next, axis=0
+            )
     values = lax.all_gather(coeffs[None], "leaf", axis=0, tiled=True)
     far_sum = lax.fori_loop(0, skeletons.shape[0], far_visit(skeletons, values), empty_far)
     upward_terms = lax.dot_general(

time: 281 us -> 263 us (0.936)
  blocking collectives: 84 us -> 64.1 us
  starting transfers between devices: 25.7 us -> 33.8 us
  local copies, waits for them, and re-layouts: 66.5 us -> 59 us
    all_gather x1 -> x0, blocking collectives: 20 us -> none  [body(): skeletons = lax.all_gather(leaf_skeleton, 'leaf', axis=0, tiled=True)]
    ppermute x0 -> x7, waiting for transfers between devices: none -> 9.41 us  [the longest x4 9.4 us: body(): e_now = ppermute(e_now, axis_name='leaf', perm=sheets)]
    ppermute x0 -> x7, starting transfers between devices: none -> 7.74 us  [the longest x4 7.43 us: body(): e_now = ppermute(e_now, axis_name='leaf', perm=sheets)]
    ppermute x6, waiting for transfers between devices: 7.31 us -> 0.02 us  [passed_along(): return lax.ppermute(block, axis, route)]
    all_gather x1, blocking collectives: 13.8 us -> 7.66 us  [body(): values = lax.all_gather(upper[None], 'group', axis=0, tiled=True)]
    dynamic_slice x8, local copies, waits for them, and re-layouts: 9.86 us -> 4.73 us  [visit(): listed = lax.dynamic_index_in_dim(far_row, position, 0, keepdims=False)]
    all_gather x1, blocking collectives: 17.8 us -> 22.4 us  [body(): values = lax.all_gather(coeffs[None], 'leaf', axis=0, tiled=True)]
    unnamed x32 -> x38, local copies, waits for them, and re-layouts: 13.4 us -> 13.3 us
  transfers between devices with their start and end apart: 6 -> 13, of which waited for: 1 -> 2; matrix products, arithmetic and copies ran while one was open for 19% -> 19% of each run, Pallas kernels for 0% -> 0%
where the time goes in v1:
time: 263 us; the launch traced here: 261 us
  blocking collectives  64.1 us (24%)
  matrix products  64 us (24%)
  local copies, waits for them, and re-layouts  59 us (22%)
  starting transfers between devices  33.8 us (13%)
  other arithmetic  17.9 us (7%)
  loops' own time  12.3 us (5%)
  waiting for transfers between devices  9.42 us (4%)
    dot_general x7, matrix products, include(): jnp.dot(kernel_tile(points, other_points), other_values, preferred_elemen...  56.5 us
    psum x1, blocking collectives, body(): upper = lax.psum(upward_terms, 'leaf').astype(jnp.bfloat16)  26.7 us
    ppermute x6, starting transfers between devices, passed_along(): return lax.ppermute(block, axis, route)  26 us
    all_gather x1, blocking collectives, body(): values = lax.all_gather(coeffs[None], 'leaf', axis=0, tiled=True)  22.4 us
    reduce_sum x10, other arithmetic, kernel_tile(): right_sq = jnp.sum(right_f * right_f, axis=1)  13.7 us
    unnamed x38, local copies, waits for them, and re-layouts  13.3 us
    while x3, local copies, waits for them, and re-layouts, body(): lax.fori_loop(0, 2 * reach + 1, window_visit, jnp.zeros((leaf_rows, rhs_c...  11.1 us
    gather x2, local copies, waits for them, and re-layouts, body(): sorted_target = target[ordering[0]]  10.2 us
  transfers between devices with their start and end apart: 13, of which 2 were waited for; matrix products, arithmetic and copies ran while one was open for 19% of the time, Pallas kernels for 0%

profile of v1, /device:TPU:15, one launch (start us, length us, event | category | flops | bytes accessed | tf_op | source)
XLA Modules:
  0.0 260.9 jit_solution(5190310139153603517)
XLA Ops:
  2.9 2.5 copy.52
  8.6 3.6 %collective-permute-start.7 = (bf16[2048,192]{0,1:T(8,128)(2,1)}, bf16[2048,192]{0,1:T(8,128)(2,1)}, u32[]{:S(2)}, u32[]{:S(2)}) collective-permute-start(bf16[2048,192]{0,1:T(8,128)(2,1)} %pad_maximum_fusion), channel_id=1, source_target_pairs={{0,1},{1,2},{2,3},{3,4},{4,5},{5,6},{6,7},{8,9},{9,10},{10,11},{11... | collective-permute-start | bytes 2359304 | tf_op jit(solution)/shard_map/ppermute | solution.py:13
  15.0 26.7 %all-reduce.1 = bf16[256,128]{0,1:T(8,128)(2,1)S(1)} all-reduce(f32[256,128]{0,1:T(8,128)S(1)} %convolution_bitcast_fusion.2), channel_id=1, replica_groups=mesh['group'=4,'leaf'=8] {'leaf'}, use_global_device_ids=true, to_apply=%region_6.7 | all-reduce | flops 32768 | bytes 196608 | tf_op jit(solution)/shard_map/psum | solution.py:140
  41.7 7.7 %all-gather.1 = bf16[1024,128]{0,1:T(8,128)(2,1)} all-gather(bf16[256,128]{0,1:T(8,128)(2,1)S(1)} %all-reduce.1), channel_id=3, replica_groups=mesh['group'=4,'leaf'=8] {'group'}, dimensions={0}, use_global_device_ids=true | all-gather | bytes 327680 | tf_op jit(solution)/shard_map/all_gather | solution.py:143
  49.4 5.5 %collective-permute-start.8 = (bf16[2048,192]{0,1:T(8,128)(2,1)}, bf16[2048,192]{0,1:T(8,128)(2,1)}, u32[]{:S(2)}, u32[]{:S(2)}) collective-permute-start(bf16[2048,192]{0,1:T(8,128)(2,1)} %collective-permute-done.7), channel_id=1, source_target_pairs={{0,1},{1,2},{2,3},{3,4},{4,5},{5,6},{6,7},{8,9},{9,10},{10,11},{11... | collective-permute-start | bytes 2359304 | tf_op jit(solution)/shard_map/ppermute | solution.py:13
  55.0 22.4 %all-gather = bf16[2048,128]{1,0:T(8,128)(2,1)} all-gather(bf16[256,128]{1,0:T(8,128)(2,1)S(1)} %convolution_convert_fusion), channel_id=2, replica_groups=mesh['group'=4,'leaf'=8] {'leaf'}, dimensions={0}, use_global_device_ids=true | all-gather | bytes 589824 | tf_op jit(solution)/shard_map/all_gather | solution.py:135
  80.4 7.4 %all_gather.10 = bf16[4,256,64]{1,2,0:T(8,128)(2,1)} all-gather(bf16[1,256,64]{1,2,0:T(8,128)(2,1)} %param.32), channel_id=1, replica_groups=mesh['group'=4,'leaf'=8] {'group'}, dimensions={0}, use_global_device_ids=true | all-gather | bytes 163840 | tf_op jit(solution)/shard_map/all_gather | solution.py:142
  89.5 7.6 %gather_fusion = f32[2048,128]{1,0:T(8,128)} fusion(f32[2048,128]{1,0:T(8,128)S(1)} %copy-done.1, s32[2048]{0:T(1024)S(1)} %broadcast_clamp_fusion), kind=kCustom, calls=%fused_computation | custom fusion | bytes 2105344 | tf_op jit(solution)/shard_map/gather | solution.py:162
  97.1 2.6 %copy.51 = f32[2048,128]{0,1:T(8,128)} copy(f32[2048,128]{1,0:T(8,128)} %gather_fusion) | data formatting | bytes 2097152 | tf_op jit(solution)/shard_map/gather | solution.py:162
  99.8 9.7 %while.51 = (s32[]{:T(128)}, f32[256,128]{1,0:T(8,128)S(1)}, s32[4]{0:T(128)S(1)}, bf16[1,256,64]{2,1,0:T(8,128)(2,1)S(1)}, bf16[4,256,64]{2,1,0:T(8,128)(2,1)},...) while((s32[]{:T(128)}, f32[256,128]{1,0:T(8,128)S(1)}, s32[4]{0:T(128)S(1)}, ...), condition=%wide.region_12.13_spmd, body=%wide.region_7.0_spmd.sunk | while | flops 25624072 | bytes 496837 | solution.py:157
  111.7 3.6 %collective-permute-start.11 = (bf16[2048,192]{0,1:T(8,128)(2,1)}, bf16[2048,192]{0,1:T(8,128)(2,1)}, u32[]{:S(2)}, u32[]{:S(2)}) collective-permute-start(bf16[2048,192]{0,1:T(8,128)(2,1)} %collective-permute-done.10), channel_id=1, source_target_pairs={{1,0},{2,1},{3,2},{4,3},{5,4},{6,5},{7,6},{9,8},{10,9},{11,10},{12... | collective-permute-start | bytes 2359304 | tf_op jit(solution)/shard_map/ppermute | solution.py:13
  120.0 7.2 %collective-permute-done.4 = bf16[1,256,64]{2,1,0:T(8,128)(2,1)S(1)} collective-permute-done((bf16[1,256,64]{2,1,0:T(8,128)(2,1)S(1)}, bf16[1,256,64]{2,1,0:T(8,128)(2,1)S(1)}, u32[]{:S(2)}, u32[]{:S(2)}) %collective-permute-start.4) | collective-permute-done | bytes 32800 | tf_op jit(solution)/shard_map/ppermute | solution.py:126
  127.2 2.6 %collective-permute-start.6 = (bf16[1,256,64]{2,1,0:T(8,128)(2,1)S(1)}, bf16[1,256,64]{2,1,0:T(8,128)(2,1)S(1)}, u32[]{:S(2)}, u32[]{:S(2)}) collective-permute-start(bf16[1,256,64]{2,1,0:T(8,128)(2,1)S(1)} %collective-permute-done.4), channel_id=1, source_target_pairs={{0,1},{1,2},{2,3},{3,4},{4,5},{5,6},{6,7},{7,0},{8,9},{9,10},{10,1... | collective-permute-start | bytes 98312 | tf_op jit(solution)/shard_map/ppermute | solution.py:126
  132.1 11.1 %while.50 = (s32[]{:T(128)}, f32[256,128]{1,0:T(8,128)S(1)}, s32[8]{0:T(128)S(1)}, bf16[1,256,64]{2,1,0:T(8,128)(2,1)S(1)}, bf16[8,256,64]{2,1,0:T(8,128)(2,1)S(...) while((s32[]{:T(128)}, f32[256,128]{1,0:T(8,128)S(1)}, s32[8]{0:T(128)S(1)}, ...), condition=%wide.region_5.6_spmd, body=%wide.region_0.5_spmd.sunk | while | flops 25624072 | bytes 529605 | solution.py:136
  144.0 9.4 %collective-permute-start.12 = (bf16[2048,192]{0,1:T(8,128)(2,1)}, bf16[2048,192]{0,1:T(8,128)(2,1)S(1)}, u32[]{:S(2)}, u32[]{:S(2)}) collective-permute-start(bf16[2048,192]{0,1:T(8,128)(2,1)} %collective-permute-done.11), channel_id=1, source_target_pairs={{1,0},{2,1},{3,2},{4,3},{5,4},{6,5},{7,6},{9,8},{10,9},{11,10},{12... | collective-permute-start | bytes 2359304 | tf_op jit(solution)/shard_map/ppermute | solution.py:13
  166.1 9.3 %copy.49 = bf16[14336,192]{1,0:T(8,128)(2,1)} copy(bf16[14336,192]{0,1:T(8,128)(2,1)} %constant_dynamic-update-slice_fusion) | data formatting | bytes 11010048 | tf_op jit(solution)/shard_map/while | solution.py:84
  176.5 77.4 %while.52 = (s32[]{:T(128)}, f32[2048,128]{1,0:T(8,128)}, s32[]{:T(128)}, s32[8]{0:T(128)S(1)}, bf16[2048,64]{1,0:T(8,128)(2,1)S(1)}, /*index=5*/bf16[14336,192]...) while((s32[]{:T(128)}, f32[2048,128]{1,0:T(8,128)}, ...), condition=%wide.region_18.19_spmd, body=%wide.region_13.18_spmd.sunk | while | flops 1632628736 | bytes 3966781 | solution.py:84
  177.9 9.8 %conditional.8 = (f32[2048,128]{1,0:T(8,128)}) conditional(s32[]{:T(128)} %convert_element_type.115, f32[2048,128]{1,0:T(8,128)} %get-tuple-element.708, (bf16[2048,64]{1,0:T(8,128)(2,1)S(1)}, s32[]{:T(128)}, bf16[14336,192]{1,0:T(8,128)(2,1)}, f32[2048,128]{1,0:T(8,128)}) %tuple.139), branch_computations={%region_14.14_spmd, %region_15.17_spmd} | conditional | flops 1632628736 | bytes 3966534 | solution.py:82
  179.5 8.1 %convolution_add_fusion = f32[2048,128]{1,0:T(8,128)} fusion(f32[2048,128]{1,0:T(8,128)} %get-tuple-element.471, bf16[2048,64]{1,0:T(8,128)(2,1)S(1)} %get-tuple-element.472, f32[2048]{0:T(1024)S(1)} %get-tuple-element.582, f32[2048]{0:T(1024)S(1)} %get-tuple-element.583, bf16[14336,192]{1,0:T(8,128)(2,1)} %get-tuple-element.473, s32[]{:T(128)S(6)} %select_n.85, ...), kind=kOutput, calls=%fused_computation.47 | convolution fusion | flops 1631846400 | bytes 3425792 | tf_op jit(solution)/shard_map/while/body/eval_jaxpr/cond/branch_1_fun/dot_general | solution.py:78
  188.9 9.8 %conditional.8 = (f32[2048,128]{1,0:T(8,128)}) conditional(s32[]{:T(128)} %convert_element_type.115, f32[2048,128]{1,0:T(8,128)} %get-tuple-element.708, (bf16[2048,64]{1,0:T(8,128)(2,1)S(1)}, s32[]{:T(128)}, bf16[14336,192]{1,0:T(8,128)(2,1)}, f32[2048,128]{1,0:T(8,128)}) %tuple.139), branch_computations={%region_14.14_spmd, %region_15.17_spmd} | conditional | flops 1632628736 | bytes 3966534 | solution.py:82
  190.6 8.1 %convolution_add_fusion = f32[2048,128]{1,0:T(8,128)} fusion(f32[2048,128]{1,0:T(8,128)} %get-tuple-element.471, bf16[2048,64]{1,0:T(8,128)(2,1)S(1)} %get-tuple-element.472, f32[2048]{0:T(1024)S(1)} %get-tuple-element.582, f32[2048]{0:T(1024)S(1)} %get-tuple-element.583, bf16[14336,192]{1,0:T(8,128)(2,1)} %get-tuple-element.473, s32[]{:T(128)S(6)} %select_n.85, ...), kind=kOutput, calls=%fused_computation.47 | convolution fusion | flops 1631846400 | bytes 3425792 | tf_op jit(solution)/shard_map/while/body/eval_jaxpr/cond/branch_1_fun/dot_general | solution.py:78
  199.9 9.8 %conditional.8 = (f32[2048,128]{1,0:T(8,128)}) conditional(s32[]{:T(128)} %convert_element_type.115, f32[2048,128]{1,0:T(8,128)} %get-tuple-element.708, (bf16[2048,64]{1,0:T(8,128)(2,1)S(1)}, s32[]{:T(128)}, bf16[14336,192]{1,0:T(8,128)(2,1)}, f32[2048,128]{1,0:T(8,128)}) %tuple.139), branch_computations={%region_14.14_spmd, %region_15.17_spmd} | conditional | flops 1632628736 | bytes 3966534 | solution.py:82
  201.6 8.1 %convolution_add_fusion = f32[2048,128]{1,0:T(8,128)} fusion(f32[2048,128]{1,0:T(8,128)} %get-tuple-element.471, bf16[2048,64]{1,0:T(8,128)(2,1)S(1)} %get-tuple-element.472, f32[2048]{0:T(1024)S(1)} %get-tuple-element.582, f32[2048]{0:T(1024)S(1)} %get-tuple-element.583, bf16[14336,192]{1,0:T(8,128)(2,1)} %get-tuple-element.473, s32[]{:T(128)S(6)} %select_n.85, ...), kind=kOutput, calls=%fused_computation.47 | convolution fusion | flops 1631846400 | bytes 3425792 | tf_op jit(solution)/shard_map/while/body/eval_jaxpr/cond/branch_1_fun/dot_general | solution.py:78
  211.0 9.8 %conditional.8 = (f32[2048,128]{1,0:T(8,128)}) conditional(s32[]{:T(128)} %convert_element_type.115, f32[2048,128]{1,0:T(8,128)} %get-tuple-element.708, (bf16[2048,64]{1,0:T(8,128)(2,1)S(1)}, s32[]{:T(128)}, bf16[14336,192]{1,0:T(8,128)(2,1)}, f32[2048,128]{1,0:T(8,128)}) %tuple.139), branch_computations={%region_14.14_spmd, %region_15.17_spmd} | conditional | flops 1632628736 | bytes 3966534 | solution.py:82
  212.7 8.1 %convolution_add_fusion = f32[2048,128]{1,0:T(8,128)} fusion(f32[2048,128]{1,0:T(8,128)} %get-tuple-element.471, bf16[2048,64]{1,0:T(8,128)(2,1)S(1)} %get-tuple-element.472, f32[2048]{0:T(1024)S(1)} %get-tuple-element.582, f32[2048]{0:T(1024)S(1)} %get-tuple-element.583, bf16[14336,192]{1,0:T(8,128)(2,1)} %get-tuple-element.473, s32[]{:T(128)S(6)} %select_n.85, ...), kind=kOutput, calls=%fused_computation.47 | convolution fusion | flops 1631846400 | bytes 3425792 | tf_op jit(solution)/shard_map/while/body/eval_jaxpr/cond/branch_1_fun/dot_general | solution.py:78
  222.0 9.8 %conditional.8 = (f32[2048,128]{1,0:T(8,128)}) conditional(s32[]{:T(128)} %convert_element_type.115, f32[2048,128]{1,0:T(8,128)} %get-tuple-element.708, (bf16[2048,64]{1,0:T(8,128)(2,1)S(1)}, s32[]{:T(128)}, bf16[14336,192]{1,0:T(8,128)(2,1)}, f32[2048,128]{1,0:T(8,128)}) %tuple.139), branch_computations={%region_14.14_spmd, %region_15.17_spmd} | conditional | flops 1632628736 | bytes 3966534 | solution.py:82
  223.7 8.1 %convolution_add_fusion = f32[2048,128]{1,0:T(8,128)} fusion(f32[2048,128]{1,0:T(8,128)} %get-tuple-element.471, bf16[2048,64]{1,0:T(8,128)(2,1)S(1)} %get-tuple-element.472, f32[2048]{0:T(1024)S(1)} %get-tuple-element.582, f32[2048]{0:T(1024)S(1)} %get-tuple-element.583, bf16[14336,192]{1,0:T(8,128)(2,1)} %get-tuple-element.473, s32[]{:T(128)S(6)} %select_n.85, ...), kind=kOutput, calls=%fused_computation.47 | convolution fusion | flops 1631846400 | bytes 3425792 | tf_op jit(solution)/shard_map/while/body/eval_jaxpr/cond/branch_1_fun/dot_general | solution.py:78
  233.1 9.8 %conditional.8 = (f32[2048,128]{1,0:T(8,128)}) conditional(s32[]{:T(128)} %convert_element_type.115, f32[2048,128]{1,0:T(8,128)} %get-tuple-element.708, (bf16[2048,64]{1,0:T(8,128)(2,1)S(1)}, s32[]{:T(128)}, bf16[14336,192]{1,0:T(8,128)(2,1)}, f32[2048,128]{1,0:T(8,128)}) %tuple.139), branch_computations={%region_14.14_spmd, %region_15.17_spmd} | conditional | flops 1632628736 | bytes 3966534 | solution.py:82
  234.7 8.1 %convolution_add_fusion = f32[2048,128]{1,0:T(8,128)} fusion(f32[2048,128]{1,0:T(8,128)} %get-tuple-element.471, bf16[2048,64]{1,0:T(8,128)(2,1)S(1)} %get-tuple-element.472, f32[2048]{0:T(1024)S(1)} %get-tuple-element.582, f32[2048]{0:T(1024)S(1)} %get-tuple-element.583, bf16[14336,192]{1,0:T(8,128)(2,1)} %get-tuple-element.473, s32[]{:T(128)S(6)} %select_n.85, ...), kind=kOutput, calls=%fused_computation.47 | convolution fusion | flops 1631846400 | bytes 3425792 | tf_op jit(solution)/shard_map/while/body/eval_jaxpr/cond/branch_1_fun/dot_general | solution.py:78
  244.1 9.8 %conditional.8 = (f32[2048,128]{1,0:T(8,128)}) conditional(s32[]{:T(128)} %convert_element_type.115, f32[2048,128]{1,0:T(8,128)} %get-tuple-element.708, (bf16[2048,64]{1,0:T(8,128)(2,1)S(1)}, s32[]{:T(128)}, bf16[14336,192]{1,0:T(8,128)(2,1)}, f32[2048,128]{1,0:T(8,128)}) %tuple.139), branch_computations={%region_14.14_spmd, %region_15.17_spmd} | conditional | flops 1632628736 | bytes 3966534 | solution.py:82
  245.8 8.1 %convolution_add_fusion = f32[2048,128]{1,0:T(8,128)} fusion(f32[2048,128]{1,0:T(8,128)} %get-tuple-element.471, bf16[2048,64]{1,0:T(8,128)(2,1)S(1)} %get-tuple-element.472, f32[2048]{0:T(1024)S(1)} %get-tuple-element.582, f32[2048]{0:T(1024)S(1)} %get-tuple-element.583, bf16[14336,192]{1,0:T(8,128)(2,1)} %get-tuple-element.473, s32[]{:T(128)S(6)} %select_n.85, ...), kind=kOutput, calls=%fused_computation.47 | convolution fusion | flops 1631846400 | bytes 3425792 | tf_op jit(solution)/shard_map/while/body/eval_jaxpr/cond/branch_1_fun/dot_general | solution.py:78
  255.5 2.9 %fusion.56 = f32[2048,128]{0,1:T(8,128)} fusion(f32[2048,128]{0,1:T(8,128)S(1)} %copy-done.2, f32[2048,128]{0,1:T(8,128)} %copy.51, f32[2048,128]{0,1:T(8,128)S(1)} %copy.50, bf16[2048,256]{1,0:T(8,128)(2,1)S(1)} %copy-done, f32[128]{0:T(128)S(1)} %copy-done.12, f32[256,128]{0,1:T(8,128)S(1)} %copy-done.8, bf16[1,256,256]{2,1,0:T(8,128)(2,1)S(1)} %copy-done.7, ...), kind=kOutput, calls=%fused_computation.58 | convolution fusion | flops 152141824 | bytes 5636608 | tf_op jit(solution)/shard_map/dot_general | solution.py:161
  (129 shorter events, 76.9 us)
Async XLA Ops:
  0.0 14.3 %copy-start = (bf16[2048,256]{1,0:T(8,128)(2,1)S(1)}, bf16[2048,256]{1,0:T(8,128)(2,1)}, u32[]{:S(2)}) copy-start(bf16[2048,256]{1,0:T(8,128)(2,1)} %param.29) | copy-start | bytes 3145732
  0.0 77.4 %copy-start.3 = (bf16[2048,64]{0,1:T(8,128)(2,1)S(1)}, bf16[2048,64]{0,1:T(8,128)(2,1)}, u32[]{:S(2)}) copy-start(bf16[2048,64]{0,1:T(8,128)(2,1)} %param.24) | copy-start | bytes 786436
  0.0 14.8 %copy-start.6 = (bf16[1,256,256]{2,1,0:T(8,128)(2,1)S(1)}, bf16[1,256,256]{2,1,0:T(8,128)(2,1)}, u32[]{:S(2)}) copy-start(bf16[1,256,256]{2,1,0:T(8,128)(2,1)} %param.30) | copy-start | bytes 393220
  0.0 55.0 %copy-start.11 = (s32[1,2048]{1,0:T(1,128)S(1)}, s32[1,2048]{1,0:T(1,128)}, u32[]{:S(2)}) copy-start(s32[1,2048]{1,0:T(1,128)} %param.25) | copy-start | bytes 24580
  1.0 88.5 %copy-start.1 = (f32[2048,128]{1,0:T(8,128)S(1)}, f32[2048,128]{1,0:T(8,128)}, u32[]{:S(2)}) copy-start(f32[2048,128]{1,0:T(8,128)} %param.27) | copy-start | bytes 3145732
  1.0 108.4 %collective-permute-start = (bf16[1,256,64]{2,1,0:T(8,128)(2,1)S(1)}, bf16[1,256,64]{2,1,0:T(8,128)(2,1)}, u32[]{:S(2)}, u32[]{:S(2)}) collective-permute-start(bf16[1,256,64]{2,1,0:T(8,128)(2,1)S(1)} %copy.43), channel_id=1, source_target_pairs={{0,1},{1,2},{2,3},{3,4},{4,5},{5,6},{6,7},{7,0},{8,9},{9,10},{10,1... | collective-permute-start | bytes 98312 | tf_op jit(solution)/shard_map/ppermute | solution.py:126
  2.9 108.4 %collective-permute-start.1 = (bf16[1,256,64]{2,1,0:T(8,128)(2,1)S(1)}, bf16[1,256,64]{2,1,0:T(8,128)(2,1)}, u32[]{:S(2)}, u32[]{:S(2)}) collective-permute-start(bf16[1,256,64]{2,1,0:T(8,128)(2,1)S(1)} %copy.43), channel_id=1, source_target_pairs={{0,7},{1,0},{2,1},{3,2},{4,3},{5,4},{6,5},{7,6},{8,15},{9,8},{10,9... | collective-permute-start | bytes 98312 | tf_op jit(solution)/shard_map/ppermute | solution.py:131
  8.6 40.8 %collective-permute-start.7 = (bf16[2048,192]{0,1:T(8,128)(2,1)}, bf16[2048,192]{0,1:T(8,128)(2,1)}, u32[]{:S(2)}, u32[]{:S(2)}) collective-permute-start(bf16[2048,192]{0,1:T(8,128)(2,1)} %pad_maximum_fusion), channel_id=1, source_target_pairs={{0,1},{1,2},{2,3},{3,4},{4,5},{5,6},{6,7},{8,9},{9,10},{10,11},{11... | collective-permute-start | bytes 2359304 | tf_op jit(solution)/shard_map/ppermute | solution.py:13
  12.3 99.4 %collective-permute-start.10 = (bf16[2048,192]{0,1:T(8,128)(2,1)}, bf16[2048,192]{0,1:T(8,128)(2,1)}, u32[]{:S(2)}, u32[]{:S(2)}) collective-permute-start(bf16[2048,192]{0,1:T(8,128)(2,1)} %pad_maximum_fusion), channel_id=1, source_target_pairs={{1,0},{2,1},{3,2},{4,3},{5,4},{6,5},{7,6},{9,8},{10,9},{11,10},{12... | collective-permute-start | bytes 2359304 | tf_op jit(solution)/shard_map/ppermute | solution.py:13
  49.4 28.0 %copy-start.4 = (bf16[8,256,64]{2,1,0:T(8,128)(2,1)}, bf16[8,256,64]{2,1,0:T(8,128)(2,1)S(1)}, u32[]{:S(2)}) copy-start(bf16[8,256,64]{2,1,0:T(8,128)(2,1)S(1)} %constant_dynamic-update-slice_fusion.14) | copy-start | bytes 786436
  49.4 65.8 %collective-permute-start.8 = (bf16[2048,192]{0,1:T(8,128)(2,1)}, bf16[2048,192]{0,1:T(8,128)(2,1)}, u32[]{:S(2)}, u32[]{:S(2)}) collective-permute-start(bf16[2048,192]{0,1:T(8,128)(2,1)} %collective-permute-done.7), channel_id=1, source_target_pairs={{0,1},{1,2},{2,3},{3,4},{4,5},{5,6},{6,7},{8,9},{9,10},{10,11},{11... | collective-permute-start | bytes 2359304 | tf_op jit(solution)/shard_map/ppermute | solution.py:13
  89.5 10.2 %copy-start.13 = (s32[1,4]{1,0:T(1,128)S(1)}, s32[1,4]{1,0:T(1,128)}, u32[]{:S(2)}) copy-start(s32[1,4]{1,0:T(1,128)} %param.35) | copy-start | bytes 52
  97.1 20.1 %copy-start.5 = (bf16[8,256,64]{2,1,0:T(8,128)(2,1)S(1)}, bf16[8,256,64]{2,1,0:T(8,128)(2,1)}, u32[]{:S(2)}) copy-start(bf16[8,256,64]{2,1,0:T(8,128)(2,1)} %copy-done.4) | copy-start | bytes 786436
  97.1 35.0 %copy-start.14 = (s32[1,8]{1,0:T(1,128)S(1)}, s32[1,8]{1,0:T(1,128)}, u32[]{:S(2)}) copy-start(s32[1,8]{1,0:T(1,128)} %param.34) | copy-start | bytes 100
  109.4 34.6 %copy-start.9 = (f32[256,128]{1,0:T(8,128)}, f32[256,128]{1,0:T(8,128)S(1)}, u32[]{:S(2)}) copy-start(f32[256,128]{1,0:T(8,128)S(1)} %get-tuple-element.486) | copy-start | bytes 393220
  109.4 9.5 %collective-permute-start.2 = (bf16[1,256,64]{2,1,0:T(8,128)(2,1)}, bf16[1,256,64]{2,1,0:T(8,128)(2,1)S(1)}, u32[]{:S(2)}, u32[]{:S(2)}) collective-permute-start(bf16[1,256,64]{2,1,0:T(8,128)(2,1)} %collective-permute-done), channel_id=1, source_target_pairs={{0,1},{1,2},{2,3},{3,4},{4,5},{5,6},{6,7},{7,0},{8,9},{9,10},{10,1... | collective-permute-start | bytes 98312 | tf_op jit(solution)/shard_map/ppermute | solution.py:126
  111.3 8.6 %collective-permute-start.3 = (bf16[1,256,64]{2,1,0:T(8,128)(2,1)}, bf16[1,256,64]{2,1,0:T(8,128)(2,1)S(1)}, u32[]{:S(2)}, u32[]{:S(2)}) collective-permute-start(bf16[1,256,64]{2,1,0:T(8,128)(2,1)} %collective-permute-done.1), channel_id=1, source_target_pairs={{0,7},{1,0},{2,1},{3,2},{4,3},{5,4},{6,5},{7,6},{8,15},{9,8},{10,9... | collective-permute-start | bytes 98312 | tf_op jit(solution)/shard_map/ppermute | solution.py:131
  111.7 32.3 %collective-permute-start.11 = (bf16[2048,192]{0,1:T(8,128)(2,1)}, bf16[2048,192]{0,1:T(8,128)(2,1)}, u32[]{:S(2)}, u32[]{:S(2)}) collective-permute-start(bf16[2048,192]{0,1:T(8,128)(2,1)} %collective-permute-done.10), channel_id=1, source_target_pairs={{1,0},{2,1},{3,2},{4,3},{5,4},{6,5},{7,6},{9,8},{10,9},{11,10},{12... | collective-permute-start | bytes 2359304 | tf_op jit(solution)/shard_map/ppermute | solution.py:13
  115.2 38.2 %collective-permute-start.9 = (bf16[2048,192]{0,1:T(8,128)(2,1)}, bf16[2048,192]{0,1:T(8,128)(2,1)}, u32[]{:S(2)}, u32[]{:S(2)}) collective-permute-start(bf16[2048,192]{0,1:T(8,128)(2,1)} %collective-permute-done.8), channel_id=1, source_target_pairs={{0,1},{1,2},{2,3},{3,4},{4,5},{5,6},{6,7},{8,9},{9,10},{10,11},{11... | collective-permute-start | bytes 2359304 | tf_op jit(solution)/shard_map/ppermute | solution.py:13
  119.0 8.2 %collective-permute-start.4 = (bf16[1,256,64]{2,1,0:T(8,128)(2,1)S(1)}, bf16[1,256,64]{2,1,0:T(8,128)(2,1)S(1)}, u32[]{:S(2)}, u32[]{:S(2)}) collective-permute-start(bf16[1,256,64]{2,1,0:T(8,128)(2,1)S(1)} %collective-permute-done.2), channel_id=1, source_target_pairs={{0,1},{1,2},{2,3},{3,4},{4,5},{5,6},{6,7},{7,0},{8,9},{9,10},{10,1... | collective-permute-start | bytes 98312 | tf_op jit(solution)/shard_map/ppermute | solution.py:126
  120.0 9.9 %collective-permute-start.5 = (bf16[1,256,64]{2,1,0:T(8,128)(2,1)S(1)}, bf16[1,256,64]{2,1,0:T(8,128)(2,1)S(1)}, u32[]{:S(2)}, u32[]{:S(2)}) collective-permute-start(bf16[1,256,64]{2,1,0:T(8,128)(2,1)S(1)} %collective-permute-done.3), channel_id=1, source_target_pairs={{0,7},{1,0},{2,1},{3,2},{4,3},{5,4},{6,5},{7,6},{8,15},{9,8},{10,9... | collective-permute-start | bytes 98312 | tf_op jit(solution)/shard_map/ppermute | solution.py:131
  127.2 4.9 %collective-permute-start.6 = (bf16[1,256,64]{2,1,0:T(8,128)(2,1)S(1)}, bf16[1,256,64]{2,1,0:T(8,128)(2,1)S(1)}, u32[]{:S(2)}, u32[]{:S(2)}) collective-permute-start(bf16[1,256,64]{2,1,0:T(8,128)(2,1)S(1)} %collective-permute-done.4), channel_id=1, source_target_pairs={{0,1},{1,2},{2,3},{3,4},{4,5},{5,6},{6,7},{7,0},{8,9},{9,10},{10,1... | collective-permute-start | bytes 98312 | tf_op jit(solution)/shard_map/ppermute | solution.py:126
  144.0 21.1 %collective-permute-start.12 = (bf16[2048,192]{0,1:T(8,128)(2,1)}, bf16[2048,192]{0,1:T(8,128)(2,1)S(1)}, u32[]{:S(2)}, u32[]{:S(2)}) collective-permute-start(bf16[2048,192]{0,1:T(8,128)(2,1)} %collective-permute-done.11), channel_id=1, source_target_pairs={{1,0},{2,1},{3,2},{4,3},{5,4},{6,5},{7,6},{9,8},{10,9},{11,10},{12... | collective-permute-start | bytes 2359304 | tf_op jit(solution)/shard_map/ppermute | solution.py:13
  166.1 10.4 %copy-start.15 = (s32[1,8]{1,0:T(1,128)S(1)}, s32[1,8]{1,0:T(1,128)}, u32[]{:S(2)}) copy-start(s32[1,8]{1,0:T(1,128)} %param.33) | copy-start | bytes 100
  176.5 78.9 %copy-start.2 = (f32[2048,128]{0,1:T(8,128)S(1)}, f32[2048,128]{0,1:T(8,128)}, u32[]{:S(2)}) copy-start(f32[2048,128]{0,1:T(8,128)} %copy.52) | copy-start | bytes 3145732
  176.5 79.0 %copy-start.7 = (bf16[1,256,256]{2,1,0:T(8,128)(2,1)S(1)}, bf16[1,256,256]{2,1,0:T(8,128)(2,1)}, u32[]{:S(2)}) copy-start(bf16[1,256,256]{2,1,0:T(8,128)(2,1)} %param.30) | copy-start | bytes 393220
  176.5 79.0 %copy-start.8 = (f32[256,128]{0,1:T(8,128)S(1)}, f32[256,128]{0,1:T(8,128)}, u32[]{:S(2)}) copy-start(f32[256,128]{0,1:T(8,128)} %copy.47) | copy-start | bytes 393220
  176.5 79.0 %copy-start.10 = (f32[256,128]{1,0:T(8,128)S(1)}, f32[256,128]{1,0:T(8,128)}, u32[]{:S(2)}) copy-start(f32[256,128]{1,0:T(8,128)} %copy-done.9) | copy-start | bytes 393220
  176.5 79.0 %copy-start.12 = (f32[128]{0:T(128)S(1)}, f32[128]{0:T(128)}, u32[]{:S(2)}) copy-start(f32[128]{0:T(128)} %param.28) | copy-start | bytes 1540
